TPU v7x, 32 devices: a whole 2x2x4 slice. The times are simulated.
32 devices in a mesh: rows: 8 (over z, y), cols: 4 (over x, core).
Axes of the slice: x: 2, y: 2, z: 4, core: 2. Of those that a mesh axis runs over, the one named last changes fastest.
Arguments:
- vectors: float32 [16384, 512], P('rows', 'cols'), may hold values from -6 to 6
- reflectors: float32 [3, 128, 256, 128], P(None, ('rows', 'cols')), may hold values from -1.05 to 1.05, as said below
- factors: float32 [3, 128, 128, 128], P(None, ('rows', 'cols')), may hold values from -0.25 to 1.1, as said below
- starts: int32 [3, 128], P(None, 'rows'), may hold values from 0 to 16256, as said below
Outputs:
- transformed: float32 [16384, 512], P('rows', 'cols')
Inputs may be any that keep to these rules, and one draw needn't show every extreme that they name: `reflectors`: each diamond's matrix is unit lower trapezoidal: entry (i, j) is 1 for i = j and 0 for i < j. `factors`: upper triangular; F is the compact-WY factor of the diamond's reflectors, the inverse of the upper triangle of V^T V with its diagonal halved, so that I - V F V^T is orthogonal. starts[t, g] lies between 128 * g and 128 * g + 64; for the first diamond and for the last diamond of every aligned block of 16 diamonds it equals 128 * g.
All inputs are finite; a program needn't handle non-finite values.
Results may differ from a plain program's by a relative error of at most 0.0003.
Values sent between devices are 32-bit elements; how exact they have to be, the bound alone decides.
A program may use at most 64 MiB of HBM per device.

v0:
```python
import jax
import jax.numpy as jnp
from jax import lax
from jax.sharding import PartitionSpec as P

TICKS = 3


highest = lax.Precision.HIGHEST


def from_behind(block, axis, distance):
    devices = range(lax.axis_size(axis))
    route = [(i - distance, i) for i in devices if i - distance in devices]
    return lax.ppermute(block, axis, route)


def product(left, right):
    return jnp.dot(left, right, precision=highest, preferred_element_type=jnp.float32)


def apply_diamond(matrix, householder, factor, start_row):
    height = householder.shape[0]
    slab_rows = lax.dynamic_slice_in_dim(matrix, start_row, height, 0)
    projected = product(householder.T, slab_rows)
    scaled = product(factor, projected)
    slab_rows = slab_rows - product(householder, scaled)
    return lax.dynamic_update_slice_in_dim(matrix, slab_rows, start_row, 0)


def on_device(vectors, reflectors, factors, starts):
    rows_here, col_count = vectors.shape
    block_size = factors.shape[-1]
    per_dev = starts.shape[1]
    row_index = lax.axis_index("rows")
    local_starts = starts - row_index * rows_here
    unit_block = jnp.eye(block_size, dtype=jnp.float32)
    zero_top = jnp.zeros((block_size, col_count), jnp.float32)
    for tick_index in range(TICKS):
        tick_refl, tick_fact = (
            lax.all_gather(reflectors[tick_index], "cols", axis=0, tiled=True),
            lax.all_gather(factors[tick_index], "cols", axis=0, tiled=True),
        )
        tick_start = local_starts[tick_index]
        upper_part = jnp.concatenate([vectors, jnp.zeros((rows_here, block_size), jnp.float32)], 1)
        lower_part = jnp.concatenate([zero_top, unit_block], 1)
        working = jnp.concatenate([upper_part, lower_part], 0)

        def apply_step(counter, matrix):
            which = per_dev - 1 - counter
            householder = lax.dynamic_index_in_dim(tick_refl, which, 0, False)
            factor = lax.dynamic_index_in_dim(tick_fact, which, 0, False)
            start_row = lax.dynamic_index_in_dim(tick_start, which, 0, False)
            return apply_diamond(matrix, householder, factor, start_row)

        working = lax.fori_loop(0, per_dev, apply_step, working)
        base_part = working[:, :col_count]
        reach_part = working[:, col_count:]
        top_map = reach_part[:block_size]
        top_value = base_part[:block_size]

        def hop_step(counter, inflow):
            outflow = top_value + product(top_map, inflow)
            return from_behind(outflow, "rows", -1)

        inflow = lax.fori_loop(0, lax.axis_size("rows") - 1, hop_step, zero_top)
        updated = base_part + product(reach_part, inflow)
        from_above = from_behind(updated[rows_here:], "rows", 1)
        head_rows = jnp.where(row_index == 0, updated[:block_size], from_above)
        vectors = jnp.concatenate([head_rows, updated[block_size:rows_here]], 0)
    return vectors


def solution(mesh):
    return jax.shard_map(
        on_device,
        mesh=mesh,
        in_specs=(
            P("rows", "cols"),
            P(None, ("rows", "cols"), None, None),
            P(None, ("rows", "cols"), None, None),
            P(None, "rows"),
        ),
        out_specs=P("rows", "cols"),
        check_vma=False,
    )
```

profile of v0, /device:TPU:0, one launch (start us, length us, event | category | flops | bytes accessed | tf_op | source)
XLA Modules:
  0.0 626.0 jit_solution(16025879864707555217)
XLA Ops:
  6.5 2.2 slice_bitcast_fusion.3
  12.3 16.1 %all-gather.15.cloned.1.call-done = f32[1,16,128,128]{3,2,0,1:T(8,128)} async-done(((f32[1,4,128,128]{3,2,0,1:T(8,128)}), f32[1,16,128,128]{3,2,0,1:T(8,128)}) %all-gather.15.cloned.1.call-update) | async-done | bytes 1048592 | tf_op jit(solution)/shard_map/all_gather | solution.py:42
  28.3 24.2 %all-gather.13.cloned.1.call-done = f32[1,16,256,128]{3,2,0,1:T(8,128)} async-done(((f32[1,4,256,128]{3,2,0,1:T(8,128)}), f32[1,16,256,128]{3,2,0,1:T(8,128)}) %all-gather.13.cloned.1.call-update) | async-done | bytes 2097168 | tf_op jit(solution)/shard_map/all_gather | solution.py:41
  52.5 132.4 %while.75 = (s32[]{:T(128)}, f32[2176,256]{1,0:T(8,128)S(1)}, s32[16]{0:T(128)S(1)}, f32[16,256,128]{2,1,0:T(8,128)}, f32[16,128,128]{2,1,0:T(8,128)}, /*index=5...) while((s32[]{:T(128)}, f32[2176,256]{1,0:T(8,128)S(1)}, s32[16]{0:T(128)S(1)}, ...), condition=%wide.region_1.2_spmd, body=%wide.region_0.1_spmd.sunk | while | flops 251723776 | bytes 2162905 | solution.py:56
  82.7 1.9 dynamic_update_slice.33
  99.4 1.9 dynamic_update_slice.33
  107.8 1.9 dynamic_update_slice.33
  116.2 1.9 dynamic_update_slice.33
  124.5 1.9 dynamic_update_slice.33
  132.9 1.9 dynamic_update_slice.33
  141.2 1.9 dynamic_update_slice.33
  149.6 1.9 dynamic_update_slice.33
  157.9 1.9 dynamic_update_slice.33
  166.3 1.9 dynamic_update_slice.33
  174.7 1.9 dynamic_update_slice.33
  185.0 49.6 %while.76 = (s32[]{:T(128)}, f32[128,128]{1,0:T(8,128)S(1)}, f32[128,128]{1,0:T(8,128)S(1)}, f32[128,128]{1,0:T(8,128)S(1)}, s32[]{:T(128)}) while((s32[]{:T(128)}, f32[128,128]{1,0:T(8,128)S(1)}, f32[128,128]{1,0:T(8,128)S(1)}, f32[128,128]{1,0:T(8,128)S(1)}, s32[]{:T(128)}) %tuple.149), condition=%wide.region_3.4_spmd, body=%wide.region_2.3_spmd.sunk | while | flops 25182208 | bytes 524389 | solution.py:66
  186.5 4.9 collective-permute-done
  192.9 5.0 collective-permute-done
  199.4 5.8 collective-permute-done
  206.7 5.8 collective-permute-done
  213.9 5.8 collective-permute-done
  221.2 6.4 %collective-permute-done = f32[128,128]{1,0:T(8,128)S(1)} collective-permute-done((f32[128,128]{1,0:T(8,128)S(1)}, f32[128,128]{1,0:T(8,128)S(1)}, u32[]{:S(2)}, u32[]{:S(2)}) %collective-permute-start) | collective-permute-done | bytes 65568 | tf_op jit(solution)/shard_map/while/body/eval_jaxpr/ppermute | solution.py:15
  229.1 5.5 collective-permute-done
  235.6 4.8 collective-permute-start.3
  242.7 128.9 %while.77 = (s32[]{:T(128)}, f32[2176,256]{1,0:T(8,128)S(1)}, s32[16]{0:T(128)S(1)}, f32[16,256,128]{2,1,0:T(8,128)}, f32[16,128,128]{2,1,0:T(8,128)}, /*index=5...) while((s32[]{:T(128)}, f32[2176,256]{1,0:T(8,128)S(1)}, s32[16]{0:T(128)S(1)}, ...), condition=%wide.region_5.6_spmd, body=%wide.region_4.5_spmd.sunk | while | flops 251723776 | bytes 2162905 | solution.py:56
  272.0 1.9 dynamic_update_slice.34
  280.1 1.9 dynamic_update_slice.34
  288.3 1.9 dynamic_update_slice.34
  296.4 1.9 dynamic_update_slice.34
  312.7 1.9 dynamic_update_slice.34
  329.0 1.9 dynamic_update_slice.34
  337.1 1.9 dynamic_update_slice.34
  345.3 1.9 dynamic_update_slice.34
  361.5 1.9 dynamic_update_slice.34
  371.6 50.8 %while.78 = (s32[]{:T(128)}, f32[128,128]{1,0:T(8,128)S(1)}, f32[128,128]{1,0:T(8,128)S(1)}, f32[128,128]{1,0:T(8,128)S(1)}, s32[]{:T(128)}) while((s32[]{:T(128)}, f32[128,128]{1,0:T(8,128)S(1)}, f32[128,128]{1,0:T(8,128)S(1)}, f32[128,128]{1,0:T(8,128)S(1)}, s32[]{:T(128)}) %tuple.155), condition=%wide.region_7.8_spmd, body=%wide.region_6.7_spmd.sunk | while | flops 25182208 | bytes 524389 | solution.py:66
  373.2 5.3 collective-permute-done.1
  380.0 5.8 collective-permute-done.1
  387.2 5.8 collective-permute-done.1
  394.6 6.2 collective-permute-done.1
  402.3 5.6 collective-permute-done.1
  409.4 5.8 collective-permute-done.1
  416.7 5.8 collective-permute-done.1
  423.5 4.8 collective-permute-start.4
  430.6 129.1 %while.79 = (s32[]{:T(128)}, f32[2176,256]{1,0:T(8,128)S(1)}, s32[16]{0:T(128)S(1)}, f32[16,256,128]{2,1,0:T(8,128)}, f32[16,128,128]{2,1,0:T(8,128)}, /*index=5...) while((s32[]{:T(128)}, f32[2176,256]{1,0:T(8,128)S(1)}, s32[16]{0:T(128)S(1)}, ...), condition=%wide.region_9.10_spmd, body=%wide.region_8.9_spmd.sunk | while | flops 251723776 | bytes 2162905 | solution.py:56
  459.9 1.9 dynamic_update_slice.35
  468.0 1.9 dynamic_update_slice.35
  476.2 1.9 dynamic_update_slice.35
  484.3 1.9 dynamic_update_slice.35
  492.5 1.9 dynamic_update_slice.35
  500.7 1.9 dynamic_update_slice.35
  508.8 1.9 dynamic_update_slice.35
  517.0 1.9 dynamic_update_slice.35
  525.1 1.9 dynamic_update_slice.35
  533.3 1.9 dynamic_update_slice.35
  541.4 1.9 dynamic_update_slice.35
  559.7 50.6 %while.80 = (s32[]{:T(128)}, f32[128,128]{1,0:T(8,128)S(1)}, f32[128,128]{1,0:T(8,128)S(1)}, f32[128,128]{1,0:T(8,128)S(1)}, s32[]{:T(128)}) while((s32[]{:T(128)}, f32[128,128]{1,0:T(8,128)S(1)}, f32[128,128]{1,0:T(8,128)S(1)}, f32[128,128]{1,0:T(8,128)S(1)}, s32[]{:T(128)}) %tuple.161), condition=%wide.region_11.12_spmd, body=%wide.region_10.11_spmd.sunk | while | flops 25182208 | bytes 524389 | solution.py:66
  561.2 5.8 collective-permute-done.2
  568.5 5.5 collective-permute-done.2
  575.5 5.8 collective-permute-done.2
  582.8 5.8 collective-permute-done.2
  590.0 5.8 collective-permute-done.2
  597.3 5.8 collective-permute-done.2
  604.6 5.8 collective-permute-done.2
  611.4 4.8 collective-permute-start.5
  (305 shorter events, 280.0 us)
Async XLA Ops:
  6.5 2.3 copy-start
  6.5 21.8 %all-gather.15.cloned.1.call-start = ((), (), s32[]{:S(2)}) async-start(), calls=%async_computation.1 | async-start | bytes 1310720 | tf_op jit(solution)/shard_map/all_gather | solution.py:42
  8.7 3.3 copy-start.2
  8.7 3.4 copy-start.1
  8.8 43.7 %all-gather.13.cloned.1.call-start = ((), (), s32[]{:S(2)}) async-start(), calls=%async_computation | async-start | bytes 2621440 | tf_op jit(solution)/shard_map/all_gather | solution.py:41
  10.1 232.6 %all-gather.19.cloned.1.call-start = ((), (), s32[]{:S(2)}) async-start(), calls=%async_computation.3 | async-start | bytes 1310720 | tf_op jit(solution)/shard_map/all_gather | solution.py:42
  10.8 231.9 %all-gather.17.cloned.1.call-start = ((), (), s32[]{:S(2)}) async-start(), calls=%async_computation.2 | async-start | bytes 2621440 | tf_op jit(solution)/shard_map/all_gather | solution.py:41
  11.4 419.2 %all-gather.23.cloned.1.call-start = ((), (), s32[]{:S(2)}) async-start(), calls=%async_computation.5 | async-start | bytes 1310720 | tf_op jit(solution)/shard_map/all_gather | solution.py:42
  12.0 418.6 %all-gather.21.cloned.1.call-start = ((), (), s32[]{:S(2)}) async-start(), calls=%async_computation.4 | async-start | bytes 2621440 | tf_op jit(solution)/shard_map/all_gather | solution.py:41
  185.2 6.2 collective-permute-start
  191.6 6.3 %collective-permute-start = (f32[128,128]{1,0:T(8,128)S(1)}, f32[128,128]{1,0:T(8,128)S(1)}, u32[]{:S(2)}, u32[]{:S(2)}) collective-permute-start(f32[128,128]{1,0:T(8,128)S(1)} %convolution_add_fusion.9), channel_id=1, source_target_pairs={{4,0},{8,4},{12,8},{16,12},{20,16},{24,20},{28,24},{5,1},{9,5},{13... | collective-permute-start | bytes 196616 | tf_op jit(solution)/shard_map/while/body/eval_jaxpr/ppermute | solution.py:15
  198.1 7.1 %collective-permute-start = (f32[128,128]{1,0:T(8,128)S(1)}, f32[128,128]{1,0:T(8,128)S(1)}, u32[]{:S(2)}, u32[]{:S(2)}) collective-permute-start(f32[128,128]{1,0:T(8,128)S(1)} %convolution_add_fusion.9), channel_id=1, source_target_pairs={{4,0},{8,4},{12,8},{16,12},{20,16},{24,20},{28,24},{5,1},{9,5},{13... | collective-permute-start | bytes 196616 | tf_op jit(solution)/shard_map/while/body/eval_jaxpr/ppermute | solution.py:15
  205.3 7.1 %collective-permute-start = (f32[128,128]{1,0:T(8,128)S(1)}, f32[128,128]{1,0:T(8,128)S(1)}, u32[]{:S(2)}, u32[]{:S(2)}) collective-permute-start(f32[128,128]{1,0:T(8,128)S(1)} %convolution_add_fusion.9), channel_id=1, source_target_pairs={{4,0},{8,4},{12,8},{16,12},{20,16},{24,20},{28,24},{5,1},{9,5},{13... | collective-permute-start | bytes 196616 | tf_op jit(solution)/shard_map/while/body/eval_jaxpr/ppermute | solution.py:15
  212.6 7.1 %collective-permute-start = (f32[128,128]{1,0:T(8,128)S(1)}, f32[128,128]{1,0:T(8,128)S(1)}, u32[]{:S(2)}, u32[]{:S(2)}) collective-permute-start(f32[128,128]{1,0:T(8,128)S(1)} %convolution_add_fusion.9), channel_id=1, source_target_pairs={{4,0},{8,4},{12,8},{16,12},{20,16},{24,20},{28,24},{5,1},{9,5},{13... | collective-permute-start | bytes 196616 | tf_op jit(solution)/shard_map/while/body/eval_jaxpr/ppermute | solution.py:15
  219.9 7.7 %collective-permute-start = (f32[128,128]{1,0:T(8,128)S(1)}, f32[128,128]{1,0:T(8,128)S(1)}, u32[]{:S(2)}, u32[]{:S(2)}) collective-permute-start(f32[128,128]{1,0:T(8,128)S(1)} %convolution_add_fusion.9), channel_id=1, source_target_pairs={{4,0},{8,4},{12,8},{16,12},{20,16},{24,20},{28,24},{5,1},{9,5},{13... | collective-permute-start | bytes 196616 | tf_op jit(solution)/shard_map/while/body/eval_jaxpr/ppermute | solution.py:15
  227.8 6.8 %collective-permute-start = (f32[128,128]{1,0:T(8,128)S(1)}, f32[128,128]{1,0:T(8,128)S(1)}, u32[]{:S(2)}, u32[]{:S(2)}) collective-permute-start(f32[128,128]{1,0:T(8,128)S(1)} %convolution_add_fusion.9), channel_id=1, source_target_pairs={{4,0},{8,4},{12,8},{16,12},{20,16},{24,20},{28,24},{5,1},{9,5},{13... | collective-permute-start | bytes 196616 | tf_op jit(solution)/shard_map/while/body/eval_jaxpr/ppermute | solution.py:15
  235.6 6.7 %collective-permute-start.3 = (f32[128,128]{1,0:T(8,128)S(1)}, f32[128,128]{1,0:T(8,128)S(1)}, u32[]{:S(2)}, u32[]{:S(2)}) collective-permute-start(f32[128,128]{1,0:T(8,128)S(1)} %slice.127), channel_id=1, source_target_pairs={{0,4},{4,8},{8,12},{12,16},{16,20},{20,24},{24,28},{1,5},{5,9},{9,... | collective-permute-start | bytes 196616 | tf_op jit(solution)/shard_map/ppermute | solution.py:15
  371.9 6.6 %collective-permute-start.1 = (f32[128,128]{1,0:T(8,128)S(1)}, f32[128,128]{1,0:T(8,128)S(1)}, u32[]{:S(2)}, u32[]{:S(2)}) collective-permute-start(f32[128,128]{1,0:T(8,128)S(1)} %convolution_add_fusion.10), channel_id=1, source_target_pairs={{4,0},{8,4},{12,8},{16,12},{20,16},{24,20},{28,24},{5,1},{9,5},{13... | collective-permute-start | bytes 196616 | tf_op jit(solution)/shard_map/while/body/eval_jaxpr/ppermute | solution.py:15
  378.7 7.1 %collective-permute-start.1 = (f32[128,128]{1,0:T(8,128)S(1)}, f32[128,128]{1,0:T(8,128)S(1)}, u32[]{:S(2)}, u32[]{:S(2)}) collective-permute-start(f32[128,128]{1,0:T(8,128)S(1)} %convolution_add_fusion.10), channel_id=1, source_target_pairs={{4,0},{8,4},{12,8},{16,12},{20,16},{24,20},{28,24},{5,1},{9,5},{13... | collective-permute-start | bytes 196616 | tf_op jit(solution)/shard_map/while/body/eval_jaxpr/ppermute | solution.py:15
  385.9 7.2 %collective-permute-start.1 = (f32[128,128]{1,0:T(8,128)S(1)}, f32[128,128]{1,0:T(8,128)S(1)}, u32[]{:S(2)}, u32[]{:S(2)}) collective-permute-start(f32[128,128]{1,0:T(8,128)S(1)} %convolution_add_fusion.10), channel_id=1, source_target_pairs={{4,0},{8,4},{12,8},{16,12},{20,16},{24,20},{28,24},{5,1},{9,5},{13... | collective-permute-start | bytes 196616 | tf_op jit(solution)/shard_map/while/body/eval_jaxpr/ppermute | solution.py:15
  393.3 7.5 %collective-permute-start.1 = (f32[128,128]{1,0:T(8,128)S(1)}, f32[128,128]{1,0:T(8,128)S(1)}, u32[]{:S(2)}, u32[]{:S(2)}) collective-permute-start(f32[128,128]{1,0:T(8,128)S(1)} %convolution_add_fusion.10), channel_id=1, source_target_pairs={{4,0},{8,4},{12,8},{16,12},{20,16},{24,20},{28,24},{5,1},{9,5},{13... | collective-permute-start | bytes 196616 | tf_op jit(solution)/shard_map/while/body/eval_jaxpr/ppermute | solution.py:15
  401.0 6.9 %collective-permute-start.1 = (f32[128,128]{1,0:T(8,128)S(1)}, f32[128,128]{1,0:T(8,128)S(1)}, u32[]{:S(2)}, u32[]{:S(2)}) collective-permute-start(f32[128,128]{1,0:T(8,128)S(1)} %convolution_add_fusion.10), channel_id=1, source_target_pairs={{4,0},{8,4},{12,8},{16,12},{20,16},{24,20},{28,24},{5,1},{9,5},{13... | collective-permute-start | bytes 196616 | tf_op jit(solution)/shard_map/while/body/eval_jaxpr/ppermute | solution.py:15
  408.1 7.1 %collective-permute-start.1 = (f32[128,128]{1,0:T(8,128)S(1)}, f32[128,128]{1,0:T(8,128)S(1)}, u32[]{:S(2)}, u32[]{:S(2)}) collective-permute-start(f32[128,128]{1,0:T(8,128)S(1)} %convolution_add_fusion.10), channel_id=1, source_target_pairs={{4,0},{8,4},{12,8},{16,12},{20,16},{24,20},{28,24},{5,1},{9,5},{13... | collective-permute-start | bytes 196616 | tf_op jit(solution)/shard_map/while/body/eval_jaxpr/ppermute | solution.py:15
  415.4 7.1 %collective-permute-start.1 = (f32[128,128]{1,0:T(8,128)S(1)}, f32[128,128]{1,0:T(8,128)S(1)}, u32[]{:S(2)}, u32[]{:S(2)}) collective-permute-start(f32[128,128]{1,0:T(8,128)S(1)} %convolution_add_fusion.10), channel_id=1, source_target_pairs={{4,0},{8,4},{12,8},{16,12},{20,16},{24,20},{28,24},{5,1},{9,5},{13... | collective-permute-start | bytes 196616 | tf_op jit(solution)/shard_map/while/body/eval_jaxpr/ppermute | solution.py:15
  423.5 6.7 %collective-permute-start.4 = (f32[128,128]{1,0:T(8,128)S(1)}, f32[128,128]{1,0:T(8,128)S(1)}, u32[]{:S(2)}, u32[]{:S(2)}) collective-permute-start(f32[128,128]{1,0:T(8,128)S(1)} %slice.130), channel_id=1, source_target_pairs={{0,4},{4,8},{8,12},{12,16},{16,20},{20,24},{24,28},{1,5},{5,9},{9,... | collective-permute-start | bytes 196616 | tf_op jit(solution)/shard_map/ppermute | solution.py:15
  559.9 7.1 %collective-permute-start.2 = (f32[128,128]{1,0:T(8,128)S(1)}, f32[128,128]{1,0:T(8,128)S(1)}, u32[]{:S(2)}, u32[]{:S(2)}) collective-permute-start(f32[128,128]{1,0:T(8,128)S(1)} %convolution_add_fusion.11), channel_id=1, source_target_pairs={{4,0},{8,4},{12,8},{16,12},{20,16},{24,20},{28,24},{5,1},{9,5},{13... | collective-permute-start | bytes 196616 | tf_op jit(solution)/shard_map/while/body/eval_jaxpr/ppermute | solution.py:15
  567.2 6.8 %collective-permute-start.2 = (f32[128,128]{1,0:T(8,128)S(1)}, f32[128,128]{1,0:T(8,128)S(1)}, u32[]{:S(2)}, u32[]{:S(2)}) collective-permute-start(f32[128,128]{1,0:T(8,128)S(1)} %convolution_add_fusion.11), channel_id=1, source_target_pairs={{4,0},{8,4},{12,8},{16,12},{20,16},{24,20},{28,24},{5,1},{9,5},{13... | collective-permute-start | bytes 196616 | tf_op jit(solution)/shard_map/while/body/eval_jaxpr/ppermute | solution.py:15
  574.2 7.1 %collective-permute-start.2 = (f32[128,128]{1,0:T(8,128)S(1)}, f32[128,128]{1,0:T(8,128)S(1)}, u32[]{:S(2)}, u32[]{:S(2)}) collective-permute-start(f32[128,128]{1,0:T(8,128)S(1)} %convolution_add_fusion.11), channel_id=1, source_target_pairs={{4,0},{8,4},{12,8},{16,12},{20,16},{24,20},{28,24},{5,1},{9,5},{13... | collective-permute-start | bytes 196616 | tf_op jit(solution)/shard_map/while/body/eval_jaxpr/ppermute | solution.py:15
  581.5 7.1 %collective-permute-start.2 = (f32[128,128]{1,0:T(8,128)S(1)}, f32[128,128]{1,0:T(8,128)S(1)}, u32[]{:S(2)}, u32[]{:S(2)}) collective-permute-start(f32[128,128]{1,0:T(8,128)S(1)} %convolution_add_fusion.11), channel_id=1, source_target_pairs={{4,0},{8,4},{12,8},{16,12},{20,16},{24,20},{28,24},{5,1},{9,5},{13... | collective-permute-start | bytes 196616 | tf_op jit(solution)/shard_map/while/body/eval_jaxpr/ppermute | solution.py:15
  588.7 7.1 %collective-permute-start.2 = (f32[128,128]{1,0:T(8,128)S(1)}, f32[128,128]{1,0:T(8,128)S(1)}, u32[]{:S(2)}, u32[]{:S(2)}) collective-permute-start(f32[128,128]{1,0:T(8,128)S(1)} %convolution_add_fusion.11), channel_id=1, source_target_pairs={{4,0},{8,4},{12,8},{16,12},{20,16},{24,20},{28,24},{5,1},{9,5},{13... | collective-permute-start | bytes 196616 | tf_op jit(solution)/shard_map/while/body/eval_jaxpr/ppermute | solution.py:15
  596.0 7.1 %collective-permute-start.2 = (f32[128,128]{1,0:T(8,128)S(1)}, f32[128,128]{1,0:T(8,128)S(1)}, u32[]{:S(2)}, u32[]{:S(2)}) collective-permute-start(f32[128,128]{1,0:T(8,128)S(1)} %convolution_add_fusion.11), channel_id=1, source_target_pairs={{4,0},{8,4},{12,8},{16,12},{20,16},{24,20},{28,24},{5,1},{9,5},{13... | collective-permute-start | bytes 196616 | tf_op jit(solution)/shard_map/while/body/eval_jaxpr/ppermute | solution.py:15
  603.3 7.1 %collective-permute-start.2 = (f32[128,128]{1,0:T(8,128)S(1)}, f32[128,128]{1,0:T(8,128)S(1)}, u32[]{:S(2)}, u32[]{:S(2)}) collective-permute-start(f32[128,128]{1,0:T(8,128)S(1)} %convolution_add_fusion.11), channel_id=1, source_target_pairs={{4,0},{8,4},{12,8},{16,12},{20,16},{24,20},{28,24},{5,1},{9,5},{13... | collective-permute-start | bytes 196616 | tf_op jit(solution)/shard_map/while/body/eval_jaxpr/ppermute | solution.py:15
  611.4 6.7 %collective-permute-start.5 = (f32[128,128]{1,0:T(8,128)S(1)}, f32[128,128]{1,0:T(8,128)S(1)}, u32[]{:S(2)}, u32[]{:S(2)}) collective-permute-start(f32[128,128]{1,0:T(8,128)S(1)} %slice.133), channel_id=1, source_target_pairs={{0,4},{4,8},{8,12},{12,16},{16,20},{20,24},{24,28},{1,5},{5,9},{9,... | collective-permute-start | bytes 196616 | tf_op jit(solution)/shard_map/ppermute | solution.py:15
Sparse Core Ops, SparseCore 0:
  8.9 19.4 all-gather.14
  29.9 22.5 all-gather.12
  54.1 16.7 all-gather.18
  72.2 22.5 all-gather.16
  96.2 16.6 all-gather.22
  240.6 20.6 all-gather.20
where the time goes:
time: 632 us; the launch traced here: 626 us
  matrix products  184 us (29%)
  waiting for transfers between devices  167 us (26%)
  local copies, waits for them, and re-layouts  121 us (19%)
  loops' own time  97.3 us (15%)
  starting transfers between devices  41.8 us (7%)
  between operations  13.8 us (2%)
    dot_general x168, matrix products, product(): jnp.dot(left, right, precision=highest, preferred_element_type=jnp.float32)  184 us
    ppermute x24, waiting for transfers between devices, from_behind(): return lax.ppermute(block, axis, route)  125 us
    another operation x3, loops' own time, on_device(): working = lax.fori_loop(0, per_dev, apply_step, working)  96.9 us
    dynamic_update_slice x48, local copies, waits for them, and re-layouts, apply_diamond(): return lax.dynamic_update_slice_in_dim(matrix, slab_rows, start_row, 0)  86.8 us
    ppermute x24, starting transfers between devices, from_behind(): return lax.ppermute(block, axis, route)  41.6 us
    dynamic_slice x48, local copies, waits for them, and re-layouts, apply_step(): start_row = lax.dynamic_index_in_dim(tick_start, which, 0, False)  30.2 us
    all_gather x3, waiting for transfers between devices, on_device(): lax.all_gather(reflectors[tick_index], 'cols', axis=0, tiled=True)  24.2 us
    all_gather x3, waiting for transfers between devices, on_device(): lax.all_gather(factors[tick_index], 'cols', axis=0, tiled=True)  16.1 us
  transfers between devices with their start and end apart: 30, of which 26 were waited for; matrix products, arithmetic and copies ran while one was open for 33% of the time, Pallas kernels for 0%

commit v1 on v0

v1 whole, which is shorter than its diff:
```python
import functools

import jax
import jax.numpy as jnp
from jax import lax
from jax.experimental import pallas as pl
from jax.experimental.pallas import tpu as pltpu
from jax.sharding import PartitionSpec as P

MESH = pl.DeviceIdType.MESH
SHIFT = 64
f32, bf16 = jnp.float32, jnp.bfloat16


def split(x):
    high = x.astype(bf16)
    return high, (x - high.astype(f32)).astype(bf16)


def dot(a, b):
    return jnp.dot(a, b, preferred_element_type=f32)


def product(a, b):
    ah, al = split(a)
    bh, bl = split(b)
    return dot(ah, bh) + (dot(al, bh) + dot(ah, bl))


def kernel(
    n_rows, n_cols,
    vec_ref, pack_ref, start_ref, out_ref,
    gat, work, vstk, wcat, inflow, head, outb, tailb,
    vec_sem, own_sem, g_send, g_recv, p_send, p_recv, f_send, f_recv,
    i_send, i_recv, h_send, h_recv,
):
    row = lax.axis_index("rows")
    col = lax.axis_index("cols")
    ticks, per, height, block = pack_ref.shape
    rows_here, width = vec_ref.shape
    n_dia = per * n_cols
    reach = height + SHIFT
    chips = n_cols // 2
    chip, core = lax.div(col, 2), lax.rem(col, 2)
    partner = chip * 2 + 1 - core
    above, below = lax.rem(row + n_rows - 1, n_rows), lax.rem(row + 1, n_rows)

    def peer_of(j):
        return lax.rem(chip + j, chips) * 2 + core

    def share(tick, owner):
        return gat.at[tick, pl.ds(owner * per, per)]

    vec_copy = pltpu.make_async_copy(
        vec_ref, work.at[pl.ds(0, rows_here), pl.ds(0, width)], vec_sem)
    vec_copy.start()

    def own_copy(tick):
        return pltpu.make_async_copy(pack_ref.at[tick], share(tick, col), own_sem.at[tick])

    barrier = pltpu.get_barrier_semaphore()
    for there in (above, below):
        pl.semaphore_signal(barrier, inc=1, device_id={"rows": there}, device_id_type=MESH)
    for j in range(1, chips):
        pl.semaphore_signal(barrier, inc=1, device_id={"cols": peer_of(j)}, device_id_type=MESH)
    pl.semaphore_signal(barrier, inc=1, device_id={"cols": partner}, device_id_type=MESH)
    pl.semaphore_wait(barrier, 2 + chips)

    def to_peer(tick, j):
        return pltpu.make_async_remote_copy(
            src_ref=pack_ref.at[tick], dst_ref=share(tick, col),
            send_sem=g_send.at[tick, j - 1], recv_sem=g_recv.at[tick, j - 1],
            device_id={"cols": peer_of(j)}, device_id_type=MESH)

    def to_partner(tick):
        return pltpu.make_async_remote_copy(
            src_ref=pack_ref.at[tick], dst_ref=share(tick, col),
            send_sem=p_send.at[tick], recv_sem=p_recv.at[tick],
            device_id={"cols": partner}, device_id_type=MESH)

    def forward(tick, j):
        owner = lax.rem(chip + chips - j, chips) * 2 + core
        return pltpu.make_async_remote_copy(
            src_ref=share(tick, owner), dst_ref=share(tick, owner),
            send_sem=f_send.at[tick, j - 1], recv_sem=f_recv.at[tick, j - 1],
            device_id={"cols": partner}, device_id_type=MESH)

    @pl.loop(0, ticks)
    def _(tick):
        for j in range(1, chips):
            to_peer(tick, j).start()
        to_partner(tick).start()
        own_copy(tick).start()

    def relay(tick):
        for j in range(1, chips):
            to_peer(tick, j).wait_recv()
            forward(tick, j).start()

    ii = lax.broadcasted_iota(jnp.int32, (block, block), 0)
    jj = lax.broadcasted_iota(jnp.int32, (block, block), 1)
    unit = jnp.where(ii == jj, 1.0, 0.0).astype(f32)
    zero = jnp.zeros((block, block), f32)
    total_rows = work.shape[0]
    left, right = pl.ds(0, width), pl.ds(width, block)

    def reset():
        work[pl.ds(rows_here, total_rows - rows_here), :] = jnp.zeros(
            (total_rows - rows_here, width + block), f32)
        work[pl.ds(rows_here, block), right] = unit

    @pl.loop(0, rows_here // block)
    def _(i):
        work[pl.ds(pl.multiple_of(i * block, block), block), right] = zero

    reset()

    def in_block(tick, k):
        return start_ref[tick, k] - row * rows_here - k * block

    def prepare(tick, k, slot):
        top = gat[tick, k, pl.ds(0, block), :]
        lower = jnp.where(ii > jj, top, unit)
        factor = jnp.where(ii <= jj, top, 0.0)
        lower = jnp.where(ii < jj, 0.0, lower)
        house = jnp.concatenate([lower, gat[tick, k, pl.ds(block, height - block), :]], 0)
        pad = jnp.zeros((2 * SHIFT, block), f32)
        house = pltpu.roll(jnp.concatenate([house, pad], 0), in_block(tick, k), 0)
        house = house[:reach]
        high, low = split(house)
        fh, fl = split(factor)
        wide = dot(high, fh) + (dot(low, fh) + dot(high, fl))
        wh, wl = split(wide)
        wcat[slot, :, pl.ds(0, block)] = wh
        wcat[slot, :, pl.ds(block, block)] = wl
        ah, al = split(house.T)
        vstk[slot, pl.ds(0, block), :] = ah
        vstk[slot, pl.ds(block, block), :] = al

    def apply(tick, k, slot):
        base = pl.multiple_of(k * block, block)
        window = pl.ds(base, reach)
        slab = work[window, :]
        vs = vstk[slot]
        wc = wcat[slot]
        sh, sl = split(slab)
        both = dot(vs, sh)
        proj = both[:block] + (both[block:] + dot(vs[:block], sl))
        ph, plow = split(proj)
        delta = dot(wc, jnp.concatenate([ph, ph], 0)) + dot(wc[:, :block], plow)
        work[window, :] = slab - delta

    def send_up(tick):
        return pltpu.make_async_remote_copy(
            src_ref=outb.at[tick], dst_ref=inflow.at[tick],
            send_sem=i_send.at[tick], recv_sem=i_recv.at[tick],
            device_id={"rows": above}, device_id_type=MESH)

    def send_down(tick):
        return pltpu.make_async_remote_copy(
            src_ref=tailb.at[tick], dst_ref=head.at[tick],
            send_sem=h_send.at[tick], recv_sem=h_recv.at[tick],
            device_id={"rows": below}, device_id_type=MESH)

    def take_head(tick):
        send_down(tick).wait_recv()
        work[pl.ds(0, block), left] = head[tick]

    vec_copy.wait()
    relay(0)

    @pl.loop(0, ticks)
    def _(tick):
        own_copy(tick).wait()
        to_partner(tick).wait_recv()
        for j in range(1, chips):
            forward(tick, j).wait_recv()

        prepare(tick, n_dia - 1, lax.rem(n_dia - 1, 2))

        @pl.loop(0, n_dia - 1)
        def _(counter):
            k = n_dia - 1 - counter
            apply(tick, k, lax.rem(k, 2))
            prepare(tick, k - 1, lax.rem(k - 1, 2))

        @pl.when(jnp.logical_and(row > 0, tick > 0))
        def _():
            take_head(tick - 1)

        apply(tick, 0, 0)

        @pl.when(row == n_rows - 1)
        def _():
            outb[tick] = work[pl.ds(0, block), left]
            send_up(tick).start()

        @pl.when(row < n_rows - 1)
        def _():
            send_up(tick).wait_recv()
            flow = inflow[tick]

            @pl.when(row > 0)
            def _():
                outb[tick] = work[pl.ds(0, block), left] + product(
                    work[pl.ds(0, block), right], flow)
                send_up(tick).start()

            tail = pl.ds(rows_here, block)
            tailb[tick] = work[tail, left] + product(work[tail, right], flow)
            send_down(tick).start()
            fh, fl = split(flow)
            fcat = jnp.concatenate([fh, fh], 0)

            @pl.loop(0, rows_here // 256)
            def _(i):
                rows = pl.ds(pl.multiple_of(i * 256, 256), 256)
                rh, rl = split(work[rows, right])
                work[rows, left] = work[rows, left] + (
                    dot(jnp.concatenate([rh, rl], 1), fcat) + dot(rh, fl))

        @pl.when(tick < ticks - 1)
        def _():
            relay(tick + 1)

            @pl.loop(0, rows_here // block)
            def _(i):
                work[pl.ds(pl.multiple_of(i * block, block), block), right] = zero
            reset()

    @pl.when(row > 0)
    def _():
        take_head(ticks - 1)

    out_copy = pltpu.make_async_copy(
        work.at[pl.ds(0, rows_here), pl.ds(0, width)], out_ref, vec_sem)
    out_copy.start()

    @pl.loop(0, ticks)
    def _(tick):
        for j in range(1, chips):
            to_peer(tick, j).wait_send()
            forward(tick, j).wait_send()
        to_partner(tick).wait_send()

        @pl.when(row > 0)
        def _():
            send_up(tick).wait_send()

        @pl.when(row < n_rows - 1)
        def _():
            send_down(tick).wait_send()

    out_copy.wait()


def solution(mesh):
    n_rows, n_cols = mesh.shape["rows"], mesh.shape["cols"]

    def on_device(vectors, reflectors, factors, starts):
        rows_here, width = vectors.shape
        ticks, per, height, block = reflectors.shape
        chips = n_cols // 2
        ii = lax.broadcasted_iota(jnp.int32, factors.shape, 2)
        jj = lax.broadcasted_iota(jnp.int32, factors.shape, 3)
        top = jnp.where(ii > jj, reflectors[:, :, :block], factors)
        packed = jnp.concatenate([top, reflectors[:, :, block:]], 2)
        dma = pltpu.SemaphoreType.DMA
        hops = max(chips - 1, 1)
        reach = height + SHIFT
        edge = (ticks, block, width)
        return pl.pallas_call(
            functools.partial(kernel, n_rows, n_cols),
            out_shape=jax.ShapeDtypeStruct(vectors.shape, f32),
            in_specs=[
                pl.BlockSpec(memory_space=pl.ANY),
                pl.BlockSpec(memory_space=pl.ANY),
                pl.BlockSpec(memory_space=pltpu.SMEM),
            ],
            out_specs=pl.BlockSpec(memory_space=pl.ANY),
            scratch_shapes=[
                pltpu.VMEM((ticks, per * n_cols, height, block), f32),
                pltpu.VMEM((rows_here + height - block + SHIFT, width + block), f32),
                pltpu.VMEM((2, 2 * block, reach), bf16),
                pltpu.VMEM((2, reach, 2 * block), bf16),
                pltpu.VMEM(edge, f32), pltpu.VMEM(edge, f32),
                pltpu.VMEM(edge, f32), pltpu.VMEM(edge, f32),
                dma, dma((ticks,)),
                dma((ticks, hops)), dma((ticks, hops)),
                dma((ticks,)), dma((ticks,)),
                dma((ticks, hops)), dma((ticks, hops)),
                dma((ticks,)), dma((ticks,)), dma((ticks,)), dma((ticks,)),
            ],
            compiler_params=pltpu.CompilerParams(
                collective_id=0, has_side_effects=True, vmem_limit_bytes=40 * 2**20),
        )(vectors, packed, starts)

    return jax.shard_map(
        on_device,
        mesh=mesh,
        in_specs=(
            P("rows", "cols"),
            P(None, ("rows", "cols"), None, None),
            P(None, ("rows", "cols"), None, None),
            P(None, "rows"),
        ),
        out_specs=P("rows", "cols"),
        check_vma=False,
    )
```

time: 632 us -> 97.3 us (0.15)
  matrix products: 184 us -> 0 us
  waiting for transfers between devices: 167 us -> 0 us
  local copies, waits for them, and re-layouts: 121 us -> 2.07 us
  loops' own time: 97.3 us -> 0 us
  Pallas kernels: 0 us -> 93.2 us
  starting transfers between devices: 41.8 us -> 0 us
  between operations: 13.8 us -> 0.04 us
    dot_general x168 -> x0, matrix products: 184 us -> none  [product(): jnp.dot(left, right, precision=highest, preferred_element_type=jnp.float32)]
    ppermute x24 -> x0, waiting for transfers between devices: 125 us -> none  [from_behind(): return lax.ppermute(block, axis, route)]
    another operation x6 -> x0, loops' own time: 97.3 us -> none  [the longest x3 96.9 us: on_device(): working = lax.fori_loop(0, per_dev, apply_step, working)]
    pallas_call x0 -> x1, Pallas kernels: none -> 93.2 us  [on_device(): pl.pallas_call(functools.partial(kernel, n_rows, n_cols), out_shape=jax.S...]
    dynamic_update_slice x48 -> x0, local copies, waits for them, and re-layouts: 86.8 us -> none  [apply_diamond(): return lax.dynamic_update_slice_in_dim(matrix, slab_rows, start_row, 0)]
    ppermute x24 -> x0, starting transfers between devices: 41.6 us -> none  [from_behind(): return lax.ppermute(block, axis, route)]
    all_gather x6 -> x0, waiting for transfers between devices: 40.3 us -> none  [the longest x3 24.2 us: on_device(): lax.all_gather(reflectors[tick_index], 'cols', axis=0, tiled=True)]
    dynamic_slice x48 -> x0, local copies, waits for them, and re-layouts: 30.2 us -> none  [apply_step(): start_row = lax.dynamic_index_in_dim(tick_start, which, 0, False)]
  transfers between devices with their start and end apart: 30 -> 0, of which waited for: 26 -> 0; matrix products, arithmetic and copies ran while one was open for 33% -> 0% of each run, Pallas kernels for 0% -> 0%
where the time goes in v1:
time: 97.3 us; the launch traced here: 97.2 us
  Pallas kernels  93.2 us (96%)
  local copies, waits for them, and re-layouts  2.07 us (2%)
  other arithmetic  1.88 us (2%)
    pallas_call x1, Pallas kernels, on_device(): pl.pallas_call(functools.partial(kernel, n_rows, n_cols), out_shape=jax.S...  93.2 us
    unnamed x5, local copies, waits for them, and re-layouts  2.07 us

profile of v1, /device:TPU:0, one launch (start us, length us, event | category | flops | bytes accessed | tf_op | source)
XLA Modules:
  0.0 97.2 jit_solution(13956256068139488013)
XLA Ops:
  0.0 1.8 %slice_select_fusion = (f32[3,4,128,128]{3,2,1,0:T(8,128)S(1)}, f32[3,4,128,128]{3,2,1,0:T(8,128)S(1)}) fusion(f32[3,4,128,128]{3,2,1,0:T(8,128)} %param.6, f32[3,4,256,128]{3,2,1,0:T(8,128)} %param.5), kind=kLoop, calls=%fused_computation.1 | loop fusion | flops 393216 | bytes 3932160 | tf_op jit(solution)/shard_map/jit(_where)/select_n | solution.py:266
  1.8 0.0 copy-start
  1.8 0.0 copy-start.1
  1.8 0.1 pad_maximum_fusion.pack_ref
  1.9 1.1 %copy-done = f32[2048,128]{1,0:T(8,128)S(1)} copy-done((f32[2048,128]{1,0:T(8,128)S(1)}, f32[2048,128]{1,0:T(8,128)}, u32[]{:S(2)}) %copy-start) | copy-done | bytes 1048600
  3.0 0.0 copy-done.1
  3.0 93.2 %shard_map.46 = f32[2048,128]{1,0:T(8,128)S(1)} custom-call(f32[2048,128]{1,0:T(8,128)S(1)} %copy-done, f32[3,4,256,128]{3,2,1,0:T(8,128)S(1)} %pad_maximum_fusion.pack_ref, s32[3,16]{1,0:T(4,128)S(1)} %copy-done.1), custom_call_target="tpu_custom_call" | custom-call | tf_op jit(solution)/shard_map/pallas_call | solution.py:272
  96.2 1.0 %copy.6 = f32[2048,128]{1,0:T(8,128)} copy(f32[2048,128]{1,0:T(8,128)S(1)} %shard_map.46) | data formatting | bytes 2097152
Async XLA Ops:
  1.8 1.2 %copy-start = (f32[2048,128]{1,0:T(8,128)S(1)}, f32[2048,128]{1,0:T(8,128)}, u32[]{:S(2)}) copy-start(f32[2048,128]{1,0:T(8,128)} %vec_ref.1) | copy-start | bytes 3145732
  1.8 1.2 %copy-start.1 = (s32[3,16]{1,0:T(4,128)S(1)}, s32[3,16]{1,0:T(4,128)}, u32[]{:S(2)}) copy-start(s32[3,16]{1,0:T(4,128)} %start_ref.1) | copy-start | bytes 580

commit v2 on v1

--- a/solution.py
+++ b/solution.py
@@ -9,6 +9,7 @@
 
 MESH = pl.DeviceIdType.MESH
 SHIFT = 64
+CHUNKS = 4
 f32, bf16 = jnp.float32, jnp.bfloat16
 
 
@@ -30,7 +31,7 @@
 def kernel(
     n_rows, n_cols,
     vec_ref, pack_ref, start_ref, out_ref,
-    gat, work, vstk, wcat, inflow, head, outb, tailb,
+    gat, work, vhi, vlo, whi, wlo, inflow, head, outb, tailb,
     vec_sem, own_sem, g_send, g_recv, p_send, p_recv, f_send, f_recv,
     i_send, i_recv, h_send, h_recv,
 ):
@@ -40,6 +41,7 @@
     rows_here, width = vec_ref.shape
     n_dia = per * n_cols
     reach = height + SHIFT
+    pairs, chunk = n_dia // 2, width // CHUNKS
     chips = n_cols // 2
     chip, core = lax.div(col, 2), lax.rem(col, 2)
     partner = chip * 2 + 1 - core
@@ -114,46 +116,59 @@
         work[pl.ds(pl.multiple_of(i * block, block), block), right] = zero
 
     reset()
+    for ref in (vhi, vlo, whi, wlo):
+        ref[...] = jnp.zeros(ref.shape, bf16)
 
     def in_block(tick, k):
         return start_ref[tick, k] - row * rows_here - k * block
 
-    def prepare(tick, k, slot):
+    def factored(tick, k):
         top = gat[tick, k, pl.ds(0, block), :]
-        lower = jnp.where(ii > jj, top, unit)
+        lower = jnp.where(ii < jj, 0.0, jnp.where(ii > jj, top, unit))
         factor = jnp.where(ii <= jj, top, 0.0)
-        lower = jnp.where(ii < jj, 0.0, lower)
-        house = jnp.concatenate([lower, gat[tick, k, pl.ds(block, height - block), :]], 0)
-        pad = jnp.zeros((2 * SHIFT, block), f32)
-        house = pltpu.roll(jnp.concatenate([house, pad], 0), in_block(tick, k), 0)
-        house = house[:reach]
-        high, low = split(house)
-        fh, fl = split(factor)
-        wide = dot(high, fh) + (dot(low, fh) + dot(high, fl))
-        wh, wl = split(wide)
-        wcat[slot, :, pl.ds(0, block)] = wh
-        wcat[slot, :, pl.ds(block, block)] = wl
-        ah, al = split(house.T)
-        vstk[slot, pl.ds(0, block), :] = ah
-        vstk[slot, pl.ds(block, block), :] = al
-
-    def apply(tick, k, slot):
-        base = pl.multiple_of(k * block, block)
-        window = pl.ds(base, reach)
+        house = jnp.concatenate(
+            [lower, gat[tick, k, pl.ds(block, height - block), :],
+             jnp.zeros((SHIFT, block), f32)], 0)
+        house = pltpu.roll(house, in_block(tick, k), 0)
+        return house, product(house, factor)
+
+    def prepare(tick, pair, slot):
+        va, wa = factored(tick, 2 * pair + 1)
+        vb, wb = factored(tick, 2 * pair)
+        va, vb = va.T, vb.T
+        overlap = reach - block
+        cross = product(vb[:, block:], wa[:overlap])
+        fix = product(wb, cross)
+        first = jnp.concatenate(
+            [-fix[:block], wa[:overlap] - fix[block:], wa[overlap:]], 0)
+        fh, fl = split(first)
+        whi[slot, :, pl.ds(0, block)] = fh
+        wlo[slot, :, pl.ds(0, block)] = fl
+        sh, sl = split(wb)
+        whi[slot, pl.ds(0, reach), pl.ds(block, block)] = sh
+        wlo[slot, pl.ds(0, reach), pl.ds(block, block)] = sl
+        ah, al = split(va)
+        vhi[slot, pl.ds(0, block), pl.ds(block, reach)] = ah
+        vlo[slot, pl.ds(0, block), pl.ds(block, reach)] = al
+        bh, bl = split(vb)
+        vhi[slot, pl.ds(block, block), pl.ds(0, reach)] = bh
+        vlo[slot, pl.ds(block, block), pl.ds(0, reach)] = bl
+
+    def apply(pair, slot):
+        window = pl.ds(pl.multiple_of(pair * 2 * block, 2 * block), reach + block)
         slab = work[window, :]
-        vs = vstk[slot]
-        wc = wcat[slot]
+        vh, vl, wh, wl = vhi[slot], vlo[slot], whi[slot], wlo[slot]
         sh, sl = split(slab)
-        both = dot(vs, sh)
-        proj = both[:block] + (both[block:] + dot(vs[:block], sl))
+        proj = dot(vh, sh) + (dot(vl, sh) + dot(vh, sl))
         ph, plow = split(proj)
-        delta = dot(wc, jnp.concatenate([ph, ph], 0)) + dot(wc[:, :block], plow)
+        delta = dot(wh, ph) + (dot(wl, ph) + dot(wh, plow))
         work[window, :] = slab - delta
 
-    def send_up(tick):
-        return pltpu.make_async_remote_copy(
-            src_ref=outb.at[tick], dst_ref=inflow.at[tick],
-            send_sem=i_send.at[tick], recv_sem=i_recv.at[tick],
+    def send_up(tick, c):
+        part = pl.ds(c * chunk, chunk)
+        return pltpu.make_async_remote_copy(
+            src_ref=outb.at[tick, part], dst_ref=inflow.at[tick, part],
+            send_sem=i_send.at[tick, c], recv_sem=i_recv.at[tick, c],
             device_id={"rows": above}, device_id_type=MESH)
 
     def send_down(tick):
@@ -176,36 +191,41 @@
         for j in range(1, chips):
             forward(tick, j).wait_recv()
 
-        prepare(tick, n_dia - 1, lax.rem(n_dia - 1, 2))
-
-        @pl.loop(0, n_dia - 1)
+        prepare(tick, pairs - 1, lax.rem(pairs - 1, 2))
+
+        @pl.loop(0, pairs - 1)
         def _(counter):
-            k = n_dia - 1 - counter
-            apply(tick, k, lax.rem(k, 2))
-            prepare(tick, k - 1, lax.rem(k - 1, 2))
+            pair = pairs - 1 - counter
+            apply(pair, lax.rem(pair, 2))
+            prepare(tick, pair - 1, lax.rem(pair - 1, 2))
 
         @pl.when(jnp.logical_and(row > 0, tick > 0))
         def _():
             take_head(tick - 1)
 
-        apply(tick, 0, 0)
+        apply(0, 0)
+        outb[tick] = work[pl.ds(0, block), left].T
 
         @pl.when(row == n_rows - 1)
         def _():
-            outb[tick] = work[pl.ds(0, block), left]
-            send_up(tick).start()
+            for c in range(CHUNKS):
+                send_up(tick, c).start()
 
         @pl.when(row < n_rows - 1)
         def _():
-            send_up(tick).wait_recv()
-            flow = inflow[tick]
-
-            @pl.when(row > 0)
-            def _():
-                outb[tick] = work[pl.ds(0, block), left] + product(
-                    work[pl.ds(0, block), right], flow)
-                send_up(tick).start()
-
+            mh, ml = split(work[pl.ds(0, block), right].T)
+            for c in range(CHUNKS):
+                send_up(tick, c).wait_recv()
+
+                @pl.when(row > 0)
+                def _():
+                    part = pl.ds(c * chunk, chunk)
+                    xh, xl = split(inflow[tick, part, :])
+                    outb[tick, part, :] = outb[tick, part, :] + (
+                        dot(xh, mh) + (dot(xl, mh) + dot(xh, ml)))
+                    send_up(tick, c).start()
+
+            flow = inflow[tick].T
             tail = pl.ds(rows_here, block)
             tailb[tick] = work[tail, left] + product(work[tail, right], flow)
             send_down(tick).start()
@@ -245,7 +265,8 @@
 
         @pl.when(row > 0)
         def _():
-            send_up(tick).wait_send()
+            for c in range(CHUNKS):
+                send_up(tick, c).wait_send()
 
         @pl.when(row < n_rows - 1)
         def _():
@@ -268,7 +289,7 @@
         dma = pltpu.SemaphoreType.DMA
         hops = max(chips - 1, 1)
         reach = height + SHIFT
-        edge = (ticks, block, width)
+        edge, flow = (ticks, block, width), (ticks, width, block)
         return pl.pallas_call(
             functools.partial(kernel, n_rows, n_cols),
             out_shape=jax.ShapeDtypeStruct(vectors.shape, f32),
@@ -281,18 +302,20 @@
             scratch_shapes=[
                 pltpu.VMEM((ticks, per * n_cols, height, block), f32),
                 pltpu.VMEM((rows_here + height - block + SHIFT, width + block), f32),
-                pltpu.VMEM((2, 2 * block, reach), bf16),
-                pltpu.VMEM((2, reach, 2 * block), bf16),
-                pltpu.VMEM(edge, f32), pltpu.VMEM(edge, f32),
-                pltpu.VMEM(edge, f32), pltpu.VMEM(edge, f32),
+                pltpu.VMEM((2, 2 * block, reach + block), bf16),
+                pltpu.VMEM((2, 2 * block, reach + block), bf16),
+                pltpu.VMEM((2, reach + block, 2 * block), bf16),
+                pltpu.VMEM((2, reach + block, 2 * block), bf16),
+                pltpu.VMEM(flow, f32), pltpu.VMEM(edge, f32),
+                pltpu.VMEM(flow, f32), pltpu.VMEM(edge, f32),
                 dma, dma((ticks,)),
                 dma((ticks, hops)), dma((ticks, hops)),
                 dma((ticks,)), dma((ticks,)),
                 dma((ticks, hops)), dma((ticks, hops)),
-                dma((ticks,)), dma((ticks,)), dma((ticks,)), dma((ticks,)),
+                dma((ticks, CHUNKS)), dma((ticks, CHUNKS)), dma((ticks,)), dma((ticks,)),
             ],
             compiler_params=pltpu.CompilerParams(
-                collective_id=0, has_side_effects=True, vmem_limit_bytes=40 * 2**20),
+                collective_id=0, has_side_effects=True, vmem_limit_bytes=60 * 2**20),
         )(vectors, packed, starts)
 
     return jax.shard_map(

time: 97.3 us -> 101 us (1.038)
  Pallas kernels: 93.2 us -> 95.3 us
  other arithmetic: 1.88 us -> 3.04 us
    pallas_call x1, Pallas kernels: 93.2 us -> 95.3 us  [on_device(): pl.pallas_call(functools.partial(kernel, n_rows, n_cols), out_shape=jax.S...]
    concatenate x1, other arithmetic: 0.11 us -> 1.28 us  [on_device(): packed = jnp.concatenate([top, reflectors[:, :, block:]], 2)]
    unnamed x5 -> x1, local copies, waits for them, and re-layouts: 2.07 us -> 2.26 us
where the time goes in v2:
time: 101 us
  Pallas kernels  95.3 us (94%)
  other arithmetic  3.04 us (3%)
  local copies, waits for them, and re-layouts  2.26 us (2%)
    pallas_call x1, Pallas kernels, on_device(): pl.pallas_call(functools.partial(kernel, n_rows, n_cols), out_shape=jax.S...  95.3 us
    unnamed x1, local copies, waits for them, and re-layouts  2.26 us

profile of v2, /device:TPU:0, one launch (start us, length us, event | category | flops | bytes accessed | tf_op | source)
XLA Modules:
  0.0 100.6 jit_solution(4387453756551851542)
XLA Ops:
  0.0 1.8 %slice_select_fusion = (f32[3,4,128,128]{3,2,1,0:T(8,128)S(1)}, f32[3,4,128,128]{3,2,1,0:T(8,128)S(1)}) fusion(f32[3,4,128,128]{3,2,1,0:T(8,128)} %param.6, f32[3,4,256,128]{3,2,1,0:T(8,128)} %param.5), kind=kLoop, calls=%fused_computation.1 | loop fusion | flops 393216 | bytes 3932160 | tf_op jit(solution)/shard_map/jit(_where)/select_n | solution.py:287
  1.8 1.3 %pad_maximum_fusion.pack_ref = f32[3,4,256,128]{3,2,1,0:T(8,128)} fusion(f32[3,4,128,128]{3,2,1,0:T(8,128)S(1)} %get-tuple-element.6, f32[3,4,128,128]{3,2,1,0:T(8,128)S(1)} %get-tuple-element.5), kind=kLoop, calls=%fused_computation | loop fusion | flops 393216 | bytes 3145728 | tf_op jit(solution)/shard_map/concatenate | solution.py:288
  3.0 95.3 %shard_map.46 = f32[2048,128]{1,0:T(8,128)} custom-call(f32[2048,128]{1,0:T(8,128)} %vec_ref.1, f32[3,4,256,128]{3,2,1,0:T(8,128)} %pad_maximum_fusion.pack_ref, s32[3,16]{1,0:T(4,128)} %start_ref.1), custom_call_target="tpu_custom_call" | custom-call | tf_op jit(solution)/shard_map/pallas_call | solution.py:293
  98.4 2.3 %copy.6 = f32[2048,128]{1,0:T(8,128)} copy(f32[2048,128]{1,0:T(8,128)} %shard_map.46) | data formatting | bytes 2097152

commit v3 on v2

--- a/solution.py
+++ b/solution.py
@@ -31,7 +31,7 @@
 def kernel(
     n_rows, n_cols,
     vec_ref, pack_ref, start_ref, out_ref,
-    gat, work, vhi, vlo, whi, wlo, inflow, head, outb, tailb,
+    gat, work, vhi, vlo, wcat, inflow, head, outb, tailb,
     vec_sem, own_sem, g_send, g_recv, p_send, p_recv, f_send, f_recv,
     i_send, i_recv, h_send, h_recv,
 ):
@@ -41,7 +41,7 @@
     rows_here, width = vec_ref.shape
     n_dia = per * n_cols
     reach = height + SHIFT
-    pairs, chunk = n_dia // 2, width // CHUNKS
+    chunk = width // CHUNKS
     chips = n_cols // 2
     chip, core = lax.div(col, 2), lax.rem(col, 2)
     partner = chip * 2 + 1 - core
@@ -116,53 +116,50 @@
         work[pl.ds(pl.multiple_of(i * block, block), block), right] = zero
 
     reset()
-    for ref in (vhi, vlo, whi, wlo):
-        ref[...] = jnp.zeros(ref.shape, bf16)
 
     def in_block(tick, k):
         return start_ref[tick, k] - row * rows_here - k * block
 
-    def factored(tick, k):
+    def prepare(tick, k):
+        slot = tick * n_dia + k
         top = gat[tick, k, pl.ds(0, block), :]
         lower = jnp.where(ii < jj, 0.0, jnp.where(ii > jj, top, unit))
-        factor = jnp.where(ii <= jj, top, 0.0)
+        fh, fl = split(jnp.where(ii <= jj, top, 0.0))
         house = jnp.concatenate(
             [lower, gat[tick, k, pl.ds(block, height - block), :],
              jnp.zeros((SHIFT, block), f32)], 0)
         house = pltpu.roll(house, in_block(tick, k), 0)
-        return house, product(house, factor)
-
-    def prepare(tick, pair, slot):
-        va, wa = factored(tick, 2 * pair + 1)
-        vb, wb = factored(tick, 2 * pair)
-        va, vb = va.T, vb.T
-        overlap = reach - block
-        cross = product(vb[:, block:], wa[:overlap])
-        fix = product(wb, cross)
-        first = jnp.concatenate(
-            [-fix[:block], wa[:overlap] - fix[block:], wa[overlap:]], 0)
-        fh, fl = split(first)
-        whi[slot, :, pl.ds(0, block)] = fh
-        wlo[slot, :, pl.ds(0, block)] = fl
-        sh, sl = split(wb)
-        whi[slot, pl.ds(0, reach), pl.ds(block, block)] = sh
-        wlo[slot, pl.ds(0, reach), pl.ds(block, block)] = sl
-        ah, al = split(va)
-        vhi[slot, pl.ds(0, block), pl.ds(block, reach)] = ah
-        vlo[slot, pl.ds(0, block), pl.ds(block, reach)] = al
-        bh, bl = split(vb)
-        vhi[slot, pl.ds(block, block), pl.ds(0, reach)] = bh
-        vlo[slot, pl.ds(block, block), pl.ds(0, reach)] = bl
-
-    def apply(pair, slot):
-        window = pl.ds(pl.multiple_of(pair * 2 * block, 2 * block), reach + block)
+        high, low = split(house)
+        wide = dot(jnp.concatenate([high, low], 1), jnp.concatenate([fh, fh], 0))
+        wh, wl = split(wide + dot(high, fl))
+        wcat[slot, :, pl.ds(0, block)] = wh
+        wcat[slot, :, pl.ds(block, block)] = wl
+        ah, al = split(house.T)
+        vhi[slot] = ah
+        vlo[slot] = al
+
+    def prepare_share(tick, owner):
+        @pl.loop(0, per, unroll=min(per, 2))
+        def _(i):
+            prepare(tick, owner * per + i)
+
+    def apply(tick, k):
+        slot = tick * n_dia + k
+        window = pl.ds(pl.multiple_of(k * block, block), reach)
+        vh, vl, wc = vhi[slot], vlo[slot], wcat[slot]
         slab = work[window, :]
-        vh, vl, wh, wl = vhi[slot], vlo[slot], whi[slot], wlo[slot]
         sh, sl = split(slab)
-        proj = dot(vh, sh) + (dot(vl, sh) + dot(vh, sl))
+        hb = block // 2
+        proj = jnp.concatenate([
+            dot(vh[p:p + hb], sh) + (dot(vl[p:p + hb], sh) + dot(vh[p:p + hb], sl))
+            for p in (0, hb)], 0)
         ph, plow = split(proj)
-        delta = dot(wh, ph) + (dot(wl, ph) + dot(wh, plow))
-        work[window, :] = slab - delta
+        pp = jnp.concatenate([ph, ph], 0)
+        hr = reach // 2
+        for p in (0, hr):
+            part = wc[p:p + hr]
+            delta = dot(part, pp) + dot(part[:, :block], plow)
+            work[pl.ds(pl.multiple_of(k * block, block) + p, hr), :] = slab[p:p + hr] - delta
 
     def send_up(tick, c):
         part = pl.ds(c * chunk, chunk)
@@ -181,29 +178,48 @@
         send_down(tick).wait_recv()
         work[pl.ds(0, block), left] = head[tick]
 
+    @pl.loop(0, 2 * ticks)
+    def _(m):
+        mine = m < ticks
+        tick = jnp.where(mine, m, m - ticks)
+
+        @pl.when(mine)
+        def _():
+            own_copy(tick).wait()
+
+        @pl.when(jnp.logical_not(mine))
+        def _():
+            to_partner(tick).wait_recv()
+
+        prepare_share(tick, jnp.where(mine, col, partner))
+
     vec_copy.wait()
     relay(0)
 
     @pl.loop(0, ticks)
     def _(tick):
-        own_copy(tick).wait()
-        to_partner(tick).wait_recv()
-        for j in range(1, chips):
-            forward(tick, j).wait_recv()
-
-        prepare(tick, pairs - 1, lax.rem(pairs - 1, 2))
-
-        @pl.loop(0, pairs - 1)
+        @pl.loop(0, 2 * (chips - 1))
+        def _(m):
+            far = m >= chips - 1
+            j = jnp.where(far, m - (chips - 1), m) + 1
+
+            @pl.when(far)
+            def _():
+                forward(tick, j).wait_recv()
+
+            owner = lax.rem(chip + chips - j, chips) * 2
+            prepare_share(tick, owner + jnp.where(far, 1 - core, core))
+
+        @pl.loop(0, n_dia - 1)
         def _(counter):
-            pair = pairs - 1 - counter
-            apply(pair, lax.rem(pair, 2))
-            prepare(tick, pair - 1, lax.rem(pair - 1, 2))
+            k = n_dia - 1 - counter
+            apply(tick, k)
 
         @pl.when(jnp.logical_and(row > 0, tick > 0))
         def _():
             take_head(tick - 1)
 
-        apply(0, 0)
+        apply(tick, 0)
         outb[tick] = work[pl.ds(0, block), left].T
 
         @pl.when(row == n_rows - 1)
@@ -302,10 +318,9 @@
             scratch_shapes=[
                 pltpu.VMEM((ticks, per * n_cols, height, block), f32),
                 pltpu.VMEM((rows_here + height - block + SHIFT, width + block), f32),
-                pltpu.VMEM((2, 2 * block, reach + block), bf16),
-                pltpu.VMEM((2, 2 * block, reach + block), bf16),
-                pltpu.VMEM((2, reach + block, 2 * block), bf16),
-                pltpu.VMEM((2, reach + block, 2 * block), bf16),
+                pltpu.VMEM((ticks * per * n_cols, block, reach), bf16),
+                pltpu.VMEM((ticks * per * n_cols, block, reach), bf16),
+                pltpu.VMEM((ticks * per * n_cols, reach, 2 * block), bf16),
                 pltpu.VMEM(flow, f32), pltpu.VMEM(edge, f32),
                 pltpu.VMEM(flow, f32), pltpu.VMEM(edge, f32),
                 dma, dma((ticks,)),

time: 101 us -> 90.2 us (0.89)
  Pallas kernels: 95.3 us -> 84.6 us
    pallas_call x1, Pallas kernels: 95.3 us -> 84.6 us  [on_device(): pl.pallas_call(functools.partial(kernel, n_rows, n_cols), out_shape=jax.S...]
where the time goes in v3:
time: 90.2 us; the launch traced here: 90 us
  Pallas kernels  84.6 us (94%)
  other arithmetic  3.04 us (3%)
  local copies, waits for them, and re-layouts  2.26 us (3%)
    pallas_call x1, Pallas kernels, on_device(): pl.pallas_call(functools.partial(kernel, n_rows, n_cols), out_shape=jax.S...  84.6 us
    unnamed x1, local copies, waits for them, and re-layouts  2.26 us

profile of v3, /device:TPU:0, one launch (start us, length us, event | category | flops | bytes accessed | tf_op | source)
XLA Modules:
  0.0 90.0 jit_solution(12472968783091731975)
XLA Ops:
  0.0 1.8 %slice_select_fusion = (f32[3,4,128,128]{3,2,1,0:T(8,128)S(1)}, f32[3,4,128,128]{3,2,1,0:T(8,128)S(1)}) fusion(f32[3,4,128,128]{3,2,1,0:T(8,128)} %param.6, f32[3,4,256,128]{3,2,1,0:T(8,128)} %param.5), kind=kLoop, calls=%fused_computation.1 | loop fusion | flops 393216 | bytes 3932160 | tf_op jit(solution)/shard_map/jit(_where)/select_n | solution.py:303
  1.8 1.3 %pad_maximum_fusion.pack_ref = f32[3,4,256,128]{3,2,1,0:T(8,128)} fusion(f32[3,4,128,128]{3,2,1,0:T(8,128)S(1)} %get-tuple-element.6, f32[3,4,128,128]{3,2,1,0:T(8,128)S(1)} %get-tuple-element.5), kind=kLoop, calls=%fused_computation | loop fusion | flops 393216 | bytes 3145728 | tf_op jit(solution)/shard_map/concatenate | solution.py:304
  3.0 84.6 %shard_map.46 = f32[2048,128]{1,0:T(8,128)} custom-call(f32[2048,128]{1,0:T(8,128)} %vec_ref.1, f32[3,4,256,128]{3,2,1,0:T(8,128)} %pad_maximum_fusion.pack_ref, s32[3,16]{1,0:T(4,128)} %start_ref.1), custom_call_target="tpu_custom_call" | custom-call | tf_op jit(solution)/shard_map/pallas_call | solution.py:309
  87.7 2.3 %copy.6 = f32[2048,128]{1,0:T(8,128)} copy(f32[2048,128]{1,0:T(8,128)} %shard_map.46) | data formatting | bytes 2097152

commit v4 on v3

--- a/solution.py
+++ b/solution.py
@@ -68,10 +68,10 @@
     pl.semaphore_signal(barrier, inc=1, device_id={"cols": partner}, device_id_type=MESH)
     pl.semaphore_wait(barrier, 2 + chips)
 
-    def to_peer(tick, j):
-        return pltpu.make_async_remote_copy(
-            src_ref=pack_ref.at[tick], dst_ref=share(tick, col),
-            send_sem=g_send.at[tick, j - 1], recv_sem=g_recv.at[tick, j - 1],
+    def to_peer(tick, j, i):
+        return pltpu.make_async_remote_copy(
+            src_ref=pack_ref.at[tick, i], dst_ref=gat.at[tick, col * per + i],
+            send_sem=g_send.at[tick, j - 1, i], recv_sem=g_recv.at[tick, j - 1, i],
             device_id={"cols": peer_of(j)}, device_id_type=MESH)
 
     def to_partner(tick):
@@ -80,24 +80,21 @@
             send_sem=p_send.at[tick], recv_sem=p_recv.at[tick],
             device_id={"cols": partner}, device_id_type=MESH)
 
-    def forward(tick, j):
+    def forward(tick, j, i):
         owner = lax.rem(chip + chips - j, chips) * 2 + core
         return pltpu.make_async_remote_copy(
-            src_ref=share(tick, owner), dst_ref=share(tick, owner),
-            send_sem=f_send.at[tick, j - 1], recv_sem=f_recv.at[tick, j - 1],
+            src_ref=gat.at[tick, owner * per + i], dst_ref=gat.at[tick, owner * per + i],
+            send_sem=f_send.at[tick, j - 1, i], recv_sem=f_recv.at[tick, j - 1, i],
             device_id={"cols": partner}, device_id_type=MESH)
 
     @pl.loop(0, ticks)
     def _(tick):
-        for j in range(1, chips):
-            to_peer(tick, j).start()
+        @pl.loop(0, per)
+        def _(m):
+            for j in range(1, chips):
+                to_peer(tick, j, per - 1 - m).start()
         to_partner(tick).start()
         own_copy(tick).start()
-
-    def relay(tick):
-        for j in range(1, chips):
-            to_peer(tick, j).wait_recv()
-            forward(tick, j).start()
 
     ii = lax.broadcasted_iota(jnp.int32, (block, block), 0)
     jj = lax.broadcasted_iota(jnp.int32, (block, block), 1)
@@ -139,7 +136,7 @@
         vlo[slot] = al
 
     def prepare_share(tick, owner):
-        @pl.loop(0, per, unroll=min(per, 2))
+        @pl.loop(0, per, unroll=1)
         def _(i):
             prepare(tick, owner * per + i)
 
@@ -194,32 +191,35 @@
         prepare_share(tick, jnp.where(mine, col, partner))
 
     vec_copy.wait()
-    relay(0)
 
     @pl.loop(0, ticks)
     def _(tick):
-        @pl.loop(0, 2 * (chips - 1))
-        def _(m):
-            far = m >= chips - 1
-            j = jnp.where(far, m - (chips - 1), m) + 1
-
-            @pl.when(far)
-            def _():
-                forward(tick, j).wait_recv()
-
-            owner = lax.rem(chip + chips - j, chips) * 2
-            prepare_share(tick, owner + jnp.where(far, 1 - core, core))
-
-        @pl.loop(0, n_dia - 1)
+        @pl.loop(0, n_dia)
         def _(counter):
             k = n_dia - 1 - counter
+            owner, i = lax.div(k, per), lax.rem(k, per)
+            o_chip, o_core = lax.div(owner, 2), lax.rem(owner, 2)
+            j = lax.rem(chip + chips - o_chip, chips)
+
+            @pl.when(j > 0)
+            def _():
+                @pl.when(o_core == 1)
+                def _():
+                    to_peer(tick, j, i).wait_recv()
+                    forward(tick, j, i).start()
+
+                @pl.when(o_core != core)
+                def _():
+                    forward(tick, j, i).wait_recv()
+
+                prepare(tick, k)
+
+            @pl.when(jnp.logical_and(k == 0, jnp.logical_and(row > 0, tick > 0)))
+            def _():
+                take_head(jnp.maximum(tick - 1, 0))
+
             apply(tick, k)
 
-        @pl.when(jnp.logical_and(row > 0, tick > 0))
-        def _():
-            take_head(tick - 1)
-
-        apply(tick, 0)
         outb[tick] = work[pl.ds(0, block), left].T
 
         @pl.when(row == n_rows - 1)
@@ -257,8 +257,6 @@
 
         @pl.when(tick < ticks - 1)
         def _():
-            relay(tick + 1)
-
             @pl.loop(0, rows_here // block)
             def _(i):
                 work[pl.ds(pl.multiple_of(i * block, block), block), right] = zero
@@ -274,9 +272,11 @@
 
     @pl.loop(0, ticks)
     def _(tick):
-        for j in range(1, chips):
-            to_peer(tick, j).wait_send()
-            forward(tick, j).wait_send()
+        @pl.loop(0, per)
+        def _(i):
+            for j in range(1, chips):
+                to_peer(tick, j, i).wait_send()
+                forward(tick, j, i).wait_send()
         to_partner(tick).wait_send()
 
         @pl.when(row > 0)
@@ -324,13 +324,13 @@
                 pltpu.VMEM(flow, f32), pltpu.VMEM(edge, f32),
                 pltpu.VMEM(flow, f32), pltpu.VMEM(edge, f32),
                 dma, dma((ticks,)),
-                dma((ticks, hops)), dma((ticks, hops)),
+                dma((ticks, hops, per)), dma((ticks, hops, per)),
                 dma((ticks,)), dma((ticks,)),
-                dma((ticks, hops)), dma((ticks, hops)),
+                dma((ticks, hops, per)), dma((ticks, hops, per)),
                 dma((ticks, CHUNKS)), dma((ticks, CHUNKS)), dma((ticks,)), dma((ticks,)),
             ],
             compiler_params=pltpu.CompilerParams(
-                collective_id=0, has_side_effects=True, vmem_limit_bytes=60 * 2**20),
+                collective_id=0, has_side_effects=True, vmem_limit_bytes=36 * 2**20),
         )(vectors, packed, starts)
 
     return jax.shard_map(

time: 90.2 us -> 85.4 us (0.947)
  Pallas kernels: 84.6 us -> 81.2 us
  other arithmetic: 3.04 us -> 1.88 us
    pallas_call x1, Pallas kernels: 84.6 us -> 81.2 us  [on_device(): pl.pallas_call(functools.partial(kernel, n_rows, n_cols), out_shape=jax.S...]
    concatenate x1, other arithmetic: 1.28 us -> 0.11 us  [on_device(): packed = jnp.concatenate([top, reflectors[:, :, block:]], 2)]
    unnamed x1 -> x5, local copies, waits for them, and re-layouts: 2.26 us -> 2.07 us
where the time goes in v4:
time: 85.4 us; the launch traced here: 85.2 us
  Pallas kernels  81.2 us (95%)
  local copies, waits for them, and re-layouts  2.07 us (2%)
  other arithmetic  1.88 us (2%)
    pallas_call x1, Pallas kernels, on_device(): pl.pallas_call(functools.partial(kernel, n_rows, n_cols), out_shape=jax.S...  81.2 us
    unnamed x5, local copies, waits for them, and re-layouts  2.07 us
    select_n x1, other arithmetic, on_device(): top = jnp.where(ii > jj, reflectors[:, :, :block], factors)  1.76 us

profile of v4, /device:TPU:0, one launch (start us, length us, event | category | flops | bytes accessed | tf_op | source)
XLA Modules:
  0.0 85.2 jit_solution(3559470932323433568)
XLA Ops:
  0.0 1.8 %slice_select_fusion = (f32[3,4,128,128]{3,2,1,0:T(8,128)S(1)}, f32[3,4,128,128]{3,2,1,0:T(8,128)S(1)}) fusion(f32[3,4,128,128]{3,2,1,0:T(8,128)} %param.6, f32[3,4,256,128]{3,2,1,0:T(8,128)} %param.5), kind=kLoop, calls=%fused_computation.1 | loop fusion | flops 393216 | bytes 3932160 | tf_op jit(solution)/shard_map/jit(_where)/select_n | solution.py:303
  1.8 0.0 copy-start
  1.8 0.0 copy-start.1
  1.8 0.1 pad_maximum_fusion.pack_ref
  1.9 1.1 %copy-done = f32[2048,128]{1,0:T(8,128)S(1)} copy-done((f32[2048,128]{1,0:T(8,128)S(1)}, f32[2048,128]{1,0:T(8,128)}, u32[]{:S(2)}) %copy-start) | copy-done | bytes 1048600
  3.0 0.0 copy-done.1
  3.0 81.2 %shard_map.46 = f32[2048,128]{1,0:T(8,128)S(1)} custom-call(f32[2048,128]{1,0:T(8,128)S(1)} %copy-done, f32[3,4,256,128]{3,2,1,0:T(8,128)S(1)} %pad_maximum_fusion.pack_ref, s32[3,16]{1,0:T(4,128)S(1)} %copy-done.1), custom_call_target="tpu_custom_call" | custom-call | tf_op jit(solution)/shard_map/pallas_call | solution.py:309
  84.2 1.0 %copy.6 = f32[2048,128]{1,0:T(8,128)} copy(f32[2048,128]{1,0:T(8,128)S(1)} %shard_map.46) | data formatting | bytes 2097152
Async XLA Ops:
  1.8 1.2 %copy-start = (f32[2048,128]{1,0:T(8,128)S(1)}, f32[2048,128]{1,0:T(8,128)}, u32[]{:S(2)}) copy-start(f32[2048,128]{1,0:T(8,128)} %vec_ref.1) | copy-start | bytes 3145732
  1.8 1.2 %copy-start.1 = (s32[3,16]{1,0:T(4,128)S(1)}, s32[3,16]{1,0:T(4,128)}, u32[]{:S(2)}) copy-start(s32[3,16]{1,0:T(4,128)} %start_ref.1) | copy-start | bytes 580

commit v5 on v4

--- a/solution.py
+++ b/solution.py
@@ -203,16 +203,23 @@
 
             @pl.when(j > 0)
             def _():
-                @pl.when(o_core == 1)
+                def relay(at):
+                    to_peer(tick, j, at).wait_recv()
+                    forward(tick, j, at).start()
+
+                @pl.when(jnp.logical_and(o_core == 1, i == per - 1))
                 def _():
-                    to_peer(tick, j, i).wait_recv()
-                    forward(tick, j, i).start()
+                    relay(i)
 
                 @pl.when(o_core != core)
                 def _():
                     forward(tick, j, i).wait_recv()
 
                 prepare(tick, k)
+
+                @pl.when(jnp.logical_and(o_core == 1, i > 0))
+                def _():
+                    relay(i - 1)
 
             @pl.when(jnp.logical_and(k == 0, jnp.logical_and(row > 0, tick > 0)))
             def _():
@@ -310,7 +317,7 @@
             functools.partial(kernel, n_rows, n_cols),
             out_shape=jax.ShapeDtypeStruct(vectors.shape, f32),
             in_specs=[
-                pl.BlockSpec(memory_space=pl.ANY),
+                pl.BlockSpec(memory_space=pltpu.MemorySpace.HBM),
                 pl.BlockSpec(memory_space=pl.ANY),
                 pl.BlockSpec(memory_space=pltpu.SMEM),
             ],

time: 85.4 us -> 86.1 us (level)
  no operation moved by 1% of the time
where the time goes in v5:
time: 86.1 us; the launch traced here: 85.9 us
  Pallas kernels  81.9 us (95%)
  local copies, waits for them, and re-layouts  2.07 us (2%)
  other arithmetic  1.88 us (2%)
    pallas_call x1, Pallas kernels, on_device(): pl.pallas_call(functools.partial(kernel, n_rows, n_cols), out_shape=jax.S...  81.9 us
    unnamed x5, local copies, waits for them, and re-layouts  2.07 us
    select_n x1, other arithmetic, on_device(): top = jnp.where(ii > jj, reflectors[:, :, :block], factors)  1.76 us

profile of v5, /device:TPU:0, one launch (start us, length us, event | category | flops | bytes accessed | tf_op | source)
XLA Modules:
  0.0 85.9 jit_solution(2335226657973868183)
XLA Ops:
  0.0 1.8 %slice_select_fusion = (f32[3,4,128,128]{3,2,1,0:T(8,128)S(1)}, f32[3,4,128,128]{3,2,1,0:T(8,128)S(1)}) fusion(f32[3,4,128,128]{3,2,1,0:T(8,128)} %param.6, f32[3,4,256,128]{3,2,1,0:T(8,128)} %param.5), kind=kLoop, calls=%fused_computation.1 | loop fusion | flops 393216 | bytes 3932160 | tf_op jit(solution)/shard_map/jit(_where)/select_n | solution.py:310
  1.8 0.0 copy-start
  1.8 0.0 copy-start.1
  1.8 0.1 pad_maximum_fusion.pack_ref
  1.9 1.1 %copy-done = f32[2048,128]{1,0:T(8,128)S(1)} copy-done((f32[2048,128]{1,0:T(8,128)S(1)}, f32[2048,128]{1,0:T(8,128)}, u32[]{:S(2)}) %copy-start) | copy-done | bytes 1048600
  3.0 0.0 copy-done.1
  3.0 81.9 %shard_map.46 = f32[2048,128]{1,0:T(8,128)S(1)} custom-call(f32[2048,128]{1,0:T(8,128)S(1)} %copy-done, f32[3,4,256,128]{3,2,1,0:T(8,128)S(1)} %pad_maximum_fusion.pack_ref, s32[3,16]{1,0:T(4,128)S(1)} %copy-done.1), custom_call_target="tpu_custom_call" | custom-call | tf_op jit(solution)/shard_map/pallas_call | solution.py:316
  84.9 1.0 %copy.6 = f32[2048,128]{1,0:T(8,128)} copy(f32[2048,128]{1,0:T(8,128)S(1)} %shard_map.46) | data formatting | bytes 2097152
Async XLA Ops:
  1.8 1.2 %copy-start = (f32[2048,128]{1,0:T(8,128)S(1)}, f32[2048,128]{1,0:T(8,128)}, u32[]{:S(2)}) copy-start(f32[2048,128]{1,0:T(8,128)} %vec_ref.1) | copy-start | bytes 3145732
  1.8 1.2 %copy-start.1 = (s32[3,16]{1,0:T(4,128)S(1)}, s32[3,16]{1,0:T(4,128)}, u32[]{:S(2)}) copy-start(s32[3,16]{1,0:T(4,128)} %start_ref.1) | copy-start | bytes 580
